TPU v7x, 256 devices: a whole 4x4x8 slice. The times are simulated.
256 devices in a mesh: wide: 32 (over y, x, core), narrow: 8 (over z).
Axes of the slice: x: 4, y: 4, z: 8, core: 2. Of those that a mesh axis runs over, the one named last changes fastest.
Arguments:
- three_centre: float32 [128, 2048, 1024], P(None, 'wide', 'narrow'), may hold values from -6 to 6
- screen_mask: int32 [128, 16, 8], P('wide', None, 'narrow'), may hold values 0 or 1
- metric: bfloat16 [1024, 1024], P(None, 'narrow'), may hold values from -0.1875 to 0.1875
Outputs:
- contracted: float32 [128, 2048, 1024], P('wide', None, 'narrow')
All inputs are finite; a program needn't handle non-finite values. No bound on the sum of `screen_mask` on one device may be relied on, other than what follows from the above.
Results may differ from a plain program's by a relative error of at most 0.0029.
Values may be sent and summed in bfloat16 or wider, within the bound.
A program may use at most 64 MiB of HBM per device.

v0:
```python
import jax
import jax.numpy as jnp
from jax import lax
from jax.sharding import PartitionSpec as P


def per_device(three_centre, screen_mask, metric):
    nub_all = screen_mask.shape[1]
    auxb_local = screen_mask.shape[2]
    remapped = lax.all_to_all(
        three_centre.astype(jnp.bfloat16), "wide", split_axis=0, concat_axis=1, tiled=True
    ).astype(three_centre.dtype)
    mu_local, nu_all, aux_local = remapped.shape
    block_rows = nu_all // nub_all
    block_cols = aux_local // auxb_local
    blocks = remapped.reshape(mu_local, nub_all, block_rows, auxb_local, block_cols)
    weights = screen_mask[:, :, None, :, None].astype(jnp.float32)
    screened = (blocks * weights).reshape(mu_local, nu_all, aux_local).astype(jnp.bfloat16)
    initial = jnp.zeros((mu_local, nu_all, metric.shape[1]), jnp.float32)
    piece = lax.all_gather(screened, "narrow", axis=2, tiled=True)
    flat = piece.reshape(-1, piece.shape[2])
    product = jnp.dot(flat, metric, preferred_element_type=jnp.float32)
    return product.reshape(initial.shape)


def solution(mesh):
    in_specs = (P(None, "wide", "narrow"), P("wide", None, "narrow"), P(None, "narrow"))
    out_specs = P("wide", None, "narrow")
    return jax.shard_map(
        per_device, mesh=mesh, in_specs=in_specs, out_specs=out_specs, check_vma=False
    )
```

profile of v0, /device:TPU:2, one launch (start us, length us, event | category | flops | bytes accessed | tf_op | source)
XLA Modules:
  0.0 246.3 jit_solution(7557963478260871547)
XLA Ops:
  6.5 0.0 copy-start
  6.5 0.0 copy-start.1
  6.5 4.1 %convert_element_type.32 = bf16[128,64,128]{2,1,0:T(8,128)(2,1)} convert(f32[128,64,128]{2,1,0:T(8,128)} %param.3) | non-fusion elementwise | flops 1048576 | bytes 6291456 | tf_op jit(solution)/shard_map/convert_element_type | solution.py:11
  10.6 7.6 %all-to-all-start = ((bf16[128,64,128]{2,1,0:T(8,128)(2,1)}), bf16[128,64,128]{2,1,0:T(8,128)(2,1)S(1)}, u32[]{:S(2)}, u32[]{:S(2)}) async-start(bf16[128,64,128]{2,1,0:T(8,128)(2,1)} %convert_element_type.32), calls=%async_computation | async-start | bytes 4194304 | tf_op jit(solution)/shard_map/all_to_all | solution.py:10
  18.2 0.0 all-gather.2.cloned.1.call-start
  18.3 0.0 copy-done.1
  18.3 0.1 broadcast_bitcast_fusion
  18.4 27.7 %all-to-all-done = bf16[128,64,128]{2,1,0:T(8,128)(2,1)S(1)} async-done(((bf16[128,64,128]{2,1,0:T(8,128)(2,1)}), bf16[128,64,128]{2,1,0:T(8,128)(2,1)S(1)}, u32[]{:S(2)}, u32[]{:S(2)}) %all-to-all-start) | async-done | bytes 2097184 | tf_op jit(solution)/shard_map/all_to_all | solution.py:10
  46.1 0.4 copy.4
  46.6 2.5 %fusion = bf16[4,2048,128]{2,1,0:T(8,128)(2,1)} fusion(f32[32,4,64,128]{3,2,0,1:T(8,128)S(1)} %copy.4, f32[4,2048]{1,0:T(4,128)S(1)} %bitcast.19), kind=kLoop, calls=%fused_computation.1 | loop fusion | flops 2097152 | bytes 6324224 | tf_op jit(solution)/shard_map/convert_element_type | solution.py:18
  49.1 0.0 all-gather.2.cloned.1.call-update
  49.1 180.2 %all-gather.2.cloned.1.call-done = bf16[4,2048,1024]{2,1,0:T(8,128)(2,1)} async-done(((bf16[4,2048,128]{2,1,0:T(8,128)(2,1)}), bf16[4,2048,1024]{2,1,0:T(8,128)(2,1)}) %all-gather.2.cloned.1.call-update) | async-done | bytes 16777232 | tf_op jit(solution)/shard_map/all_gather | solution.py:20
  229.3 0.0 copy-done
  229.3 10.1 %fusion.1 = f32[4,2048,128]{2,1,0:T(8,128)} fusion(bf16[4,2048,1024]{2,1,0:T(8,128)(2,1)} %all-gather.2.cloned.1.call-done, bf16[1024,128]{1,0:T(8,128)(2,1)S(1)} %copy-done), kind=kOutput, calls=%fused_computation.2 | convolution fusion | flops 2147483648 | bytes 21233664 | tf_op jit(solution)/shard_map/dot_general | solution.py:22
  (2 shorter events, 0.0 us)
Async XLA Ops:
  6.5 222.8 %copy-start = (bf16[1024,128]{1,0:T(8,128)(2,1)S(1)}, bf16[1024,128]{1,0:T(8,128)(2,1)}, u32[]{:S(2)}) copy-start(bf16[1024,128]{1,0:T(8,128)(2,1)} %param.5) | copy-start | bytes 786436
  6.5 11.7 %copy-start.1 = (s32[4,16,1]{1,2,0:T(1,128)S(1)}, s32[4,16,1]{1,2,0:T(1,128)}, u32[]{:S(2)}) copy-start(s32[4,16,1]{1,2,0:T(1,128)} %param.4) | copy-start | bytes 772
  10.6 35.5 %all-to-all-start = ((bf16[128,64,128]{2,1,0:T(8,128)(2,1)}), bf16[128,64,128]{2,1,0:T(8,128)(2,1)S(1)}, u32[]{:S(2)}, u32[]{:S(2)}) async-start(bf16[128,64,128]{2,1,0:T(8,128)(2,1)} %convert_element_type.32), calls=%async_computation | async-start | bytes 4194304 | tf_op jit(solution)/shard_map/all_to_all | solution.py:10
  18.2 211.1 %all-gather.2.cloned.1.call-start = ((), (), s32[]{:S(2)}) async-start(), calls=%async_computation.1 | async-start | bytes 18874368 | tf_op jit(solution)/shard_map/all_gather | solution.py:20
Sparse Core Ops, SparseCore 0:
  49.2 180.0 all-gather.1
where the time goes:
time: 246 us
  waiting for transfers between devices  208 us (85%)
  between operations  13.4 us (5%)
  matrix products  10.1 us (4%)
  starting transfers between devices  7.66 us (3%)
  other arithmetic  6.57 us (3%)
    all_gather x1, waiting for transfers between devices, per_device(): piece = lax.all_gather(screened, 'narrow', axis=2, tiled=True)  180 us
    all_to_all x1, waiting for transfers between devices, per_device(): lax.all_to_all(three_centre.astype(jnp.bfloat16), 'wide', split_axis=0, c...  27.7 us
    dot_general x1, matrix products, per_device(): product = jnp.dot(flat, metric, preferred_element_type=jnp.float32)  10.1 us
    all_to_all x1, starting transfers between devices, per_device(): lax.all_to_all(three_centre.astype(jnp.bfloat16), 'wide', split_axis=0, c...  7.62 us
  transfers between devices with their start and end apart: 2, of which 2 were waited for; matrix products, arithmetic and copies ran while one was open for 0% of the time, Pallas kernels for 0%

commit v1 on v0

v1 whole, which is shorter than its diff:
```python
import jax
import jax.numpy as jnp
from jax import lax
from jax.experimental import pallas as pl
from jax.experimental.pallas import tpu as pltpu
from jax.sharding import PartitionSpec as P

MESH = pl.DeviceIdType.MESH
BF = jnp.bfloat16
F32 = jnp.float32
SIDE, CORES, DEPTH = 4, 2, 8
WIDE = SIDE * SIDE * CORES
CHIPS = SIDE * SIDE
LANES = 128
PAIR = 2

OFFSETS = (
    (0, 0), (1, 0), (-1, 0), (0, 1), (0, -1), (1, 1), (-1, -1), (-1, 1),
    (1, -1), (2, 0), (0, 2), (2, 1), (1, 2), (2, -1), (-1, 2), (2, 2),
)
Z_ORDER = (4, 3, 5, 2, 6, 1, 7)
METRIC_FROM = 4


def pick(index, table):
    total = jnp.int32(0)
    for k, value in enumerate(table):
        if value:
            total = total + jnp.where(index == k, jnp.int32(value), jnp.int32(0))
    return total


def body(
    x_ref, mask_ref, metric_ref, out_ref,
    xf, xb, rb, sb, ab, mb, yb,
    load_sem, own_sem, s1_send, s1_recv, a_send, a_recv, b_send, b_recv,
    mz_send, mz_recv, mm_send, mm_recv, mc_send, mc_recv,
):
    w = lax.axis_index("wide")
    z = lax.axis_index("narrow")
    core = lax.rem(w, 2)
    xx = lax.rem(w // 2, SIDE)
    yy = w // (2 * SIDE)
    half, quarter = z // 4, lax.rem(z, 4)

    def chip_at(dx, dy):
        return lax.rem(yy + dy + SIDE, SIDE) * SIDE + lax.rem(xx + dx + SIDE, SIDE)

    def load(g):
        dx, dy = OFFSETS[g]
        rows = pl.ds(chip_at(dx, dy) * 8, 8)
        return pltpu.make_async_copy(x_ref.at[rows], xf.at[rows], load_sem.at[g])

    for g in range(CHIPS):
        load(g).start()

    barrier = pltpu.get_barrier_semaphore()
    for k in range(1, DEPTH):
        pl.semaphore_signal(
            barrier, inc=1, device_id=(w, lax.rem(z + k, DEPTH)), device_id_type=MESH
        )
    for g in range(CHIPS):
        dx, dy = OFFSETS[g]
        for dc in (0, 1):
            if g == 0 and dc == 0:
                continue
            pl.semaphore_signal(
                barrier, inc=1,
                device_id=(chip_at(dx, dy) * 2 + lax.rem(core + dc, 2), z),
                device_id_type=MESH,
            )

    def convert(g):
        dx, dy = OFFSETS[g]
        first = chip_at(dx, dy) * 8
        load(g).wait()
        xb[pl.ds(first, 8)] = xf[pl.ds(first, 8)].astype(BF)

    convert(0)
    convert(1)
    pl.semaphore_wait(barrier, DEPTH - 1 + WIDE - 1)

    my_rows = pl.ds(pl.multiple_of(w * 32, 32), 32)
    my_lanes = pl.ds(pl.multiple_of(z * LANES, LANES), LANES)
    pltpu.make_async_copy(metric_ref.at[my_rows], mb.at[w, :, my_lanes], mz_recv).start()
    for k in Z_ORDER:
        pltpu.make_async_remote_copy(
            metric_ref.at[my_rows], mb.at[w, :, my_lanes], mz_send, mz_recv,
            device_id=(w, lax.rem(z + k, DEPTH)), device_id_type=MESH,
        ).start()

    def plane_send(g):
        dx, dy = OFFSETS[g]
        chip = chip_at(dx, dy)
        if g == 0:
            pltpu.make_async_copy(xb.at[pl.ds(w * 4, 4)], rb.at[0, core], s1_recv.at[0]).start()
        for dc in (0, 1):
            if g == 0 and dc == 0:
                continue
            there = chip * 2 + lax.rem(core + dc, 2)
            pltpu.make_async_remote_copy(
                xb.at[pl.ds(there * 4, 4)], rb.at[g, core], s1_send, s1_recv.at[g],
                device_id=(there, z), device_id_type=MESH,
            ).start()

    def metric_send(g):
        dx, dy = OFFSETS[g]
        pltpu.make_async_remote_copy(
            mb.at[w], mb.at[w], mm_send, mm_recv.at[g],
            device_id=(chip_at(dx, dy) * 2 + core, z), device_id_type=MESH,
        ).start()

    def metric_across(source):
        pltpu.make_async_remote_copy(
            mb.at[source], mb.at[source], mc_send, mc_recv,
            device_id=(w + 1 - 2 * core, z), device_id_type=MESH,
        ).start()

    for g in range(CHIPS):
        if g + 2 < CHIPS:
            convert(g + 2)
        plane_send(g)
        if g == METRIC_FROM:
            pltpu.make_async_copy(mb.at[w], mb.at[w], mz_recv).wait()
            metric_across(w)
        if g > METRIC_FROM:
            metric_send(g - METRIC_FROM)
    for g in range(CHIPS - METRIC_FROM, CHIPS):
        metric_send(g)

    def screen(g):
        dx, dy = OFFSETS[g]
        chip = chip_at(-dx, -dy)
        pltpu.make_async_copy(rb.at[g], rb.at[g], s1_recv.at[g]).wait()
        for m in range(4):
            weight = mask_ref[m, chip].astype(F32)
            for c in range(CORES):
                piece = (rb[g, c, m].astype(F32) * weight).astype(BF)
                sb[g, pl.ds((m // 2) * 4, 4), m % 2, c] = piece.reshape(4, 16, LANES)

    def deep_send(g):
        pltpu.make_async_copy(sb.at[g, z], ab.at[g, :, :, :, my_lanes], a_recv.at[g]).start()
        for k in Z_ORDER:
            there = lax.rem(z + k, DEPTH)
            pltpu.make_async_remote_copy(
                sb.at[g, there], ab.at[g, :, :, :, my_lanes], a_send, a_recv.at[g],
                device_id=(w, there), device_id_type=MESH,
            ).start()

    for g in range(CHIPS):
        screen(g)
        if g >= 1:
            deep_send(g - 1)
        if g > METRIC_FROM:
            k = g - METRIC_FROM
            dx, dy = OFFSETS[k]
            source = chip_at(-dx, -dy) * 2 + core
            pltpu.make_async_copy(mb.at[source], mb.at[source], mm_recv.at[k]).wait()
            metric_across(source)
    deep_send(CHIPS - 1)
    for k in range(CHIPS - METRIC_FROM, CHIPS):
        dx, dy = OFFSETS[k]
        source = chip_at(-dx, -dy) * 2 + core
        pltpu.make_async_copy(mb.at[source], mb.at[source], mm_recv.at[k]).wait()
        metric_across(source)
    pltpu.make_async_copy(mb.at[pl.ds(0, CHIPS)], mb.at[pl.ds(0, CHIPS)], mc_recv).wait()

    dxs = [dx % SIDE for dx, _ in OFFSETS]
    dys = [dy % SIDE for _, dy in OFFSETS]

    def result_send(g):
        xs = lax.rem(xx - pick(g, dxs) + SIDE, SIDE)
        ys = lax.rem(yy - pick(g, dys) + SIDE, SIDE)
        place = out_ref.at[pl.ds(half * 2, 2), ys, xs, :, quarter]
        pltpu.make_async_copy(yb.at[g, :, :, :, my_lanes], place, b_recv).start()
        for k in Z_ORDER:
            there = lax.rem(z + k, DEPTH)
            lanes = pl.ds(pl.multiple_of(there * LANES, LANES), LANES)
            pltpu.make_async_remote_copy(
                yb.at[g, :, :, :, lanes], place, b_send, b_recv,
                device_id=(w, there), device_id_type=MESH,
            ).start()

    def contract(step):
        for i in range(PAIR):
            g = step * PAIR + i
            pltpu.make_async_copy(ab.at[g], ab.at[g], a_recv.at[g]).wait()
        rows = ab[pl.ds(step * PAIR, PAIR)].reshape(PAIR * 64, 1024)
        product = jnp.dot(rows, mb[...].reshape(1024, 1024), preferred_element_type=F32)
        yb[pl.ds(step * PAIR, PAIR)] = product.astype(BF).reshape(PAIR, 2, 2, 16, 1024)

    contract(0)

    @pl.loop(1, CHIPS // PAIR)
    def _(step):
        contract(step)
        for i in range(PAIR):
            result_send((step - 1) * PAIR + i)

    for i in range(PAIR):
        result_send(CHIPS - PAIR + i)

    def drain(ref, sem):
        pltpu.make_async_copy(ref, ref, sem).wait()

    drain(xb.at[pl.ds(0, 124)], s1_send)
    drain(mb.at[0, :, pl.ds(0, 7 * LANES)], mz_send)
    drain(mb.at[pl.ds(0, 15)], mm_send)
    drain(mb.at[pl.ds(0, 16)], mc_send)
    drain(sb.at[:, pl.ds(0, 7)], a_send)
    drain(yb.at[:, :, :, :, pl.ds(0, 7 * LANES)], b_send)
    drain(out_ref, b_recv)


def per_device(three_centre, screen_mask, metric):
    dma = pltpu.SemaphoreType.DMA
    result = pl.pallas_call(
        body,
        out_shape=jax.ShapeDtypeStruct((4, SIDE, SIDE, CORES, 4, 16, LANES), BF),
        in_specs=[
            pl.BlockSpec(memory_space=pl.ANY),
            pl.BlockSpec(memory_space=pltpu.SMEM),
            pl.BlockSpec(memory_space=pl.ANY),
        ],
        out_specs=pl.BlockSpec(memory_space=pl.ANY),
        scratch_shapes=[
            pltpu.VMEM((128, 64, LANES), F32),
            pltpu.VMEM((128, 64, LANES), BF),
            pltpu.VMEM((CHIPS, CORES, 4, 64, LANES), BF),
            pltpu.VMEM((CHIPS, DEPTH, 2, 2, 16, LANES), BF),
            pltpu.VMEM((CHIPS, 2, 2, 16, 1024), BF),
            pltpu.VMEM((WIDE, 32, 1024), BF),
            pltpu.VMEM((CHIPS, 2, 2, 16, 1024), BF),
            dma((CHIPS,)), dma, dma, dma((CHIPS,)), dma, dma((CHIPS,)), dma, dma,
            dma, dma, dma, dma((CHIPS,)), dma, dma,
        ],
        compiler_params=pltpu.CompilerParams(
            collective_id=0, has_side_effects=True, vmem_limit_bytes=56 * 1024 * 1024
        ),
        name="screen_contract",
    )(three_centre, screen_mask.reshape(4, 16), metric)
    return result.reshape(4, 2048, LANES).astype(F32)


def solution(mesh):
    in_specs = (P(None, "wide", "narrow"), P("wide", None, "narrow"), P(None, "narrow"))
    out_specs = P("wide", None, "narrow")
    return jax.shard_map(
        per_device, mesh=mesh, in_specs=in_specs, out_specs=out_specs, check_vma=False
    )
```

time: 246 us -> 113 us (0.46)
  waiting for transfers between devices: 208 us -> 0 us
  Pallas kernels: 0 us -> 109 us
  between operations: 13.4 us -> 0.01 us
  matrix products: 10.1 us -> 0 us
  starting transfers between devices: 7.66 us -> 0 us
  other arithmetic: 6.57 us -> 3.88 us
    all_gather x1 -> x0, waiting for transfers between devices: 180 us -> none  [per_device(): piece = lax.all_gather(screened, 'narrow', axis=2, tiled=True)]
    pallas_call x0 -> x1, Pallas kernels: none -> 109 us  [per_device(): pl.pallas_call(body, out_shape=jax.ShapeDtypeStruct((4, SIDE, SIDE, CORES...]
    all_to_all x1 -> x0, waiting for transfers between devices: 27.7 us -> none  [per_device(): lax.all_to_all(three_centre.astype(jnp.bfloat16), 'wide', split_axis=0, c...]
    dot_general x1 -> x0, matrix products: 10.1 us -> none  [per_device(): product = jnp.dot(flat, metric, preferred_element_type=jnp.float32)]
    all_to_all x1 -> x0, starting transfers between devices: 7.62 us -> none  [per_device(): lax.all_to_all(three_centre.astype(jnp.bfloat16), 'wide', split_axis=0, c...]
    convert_element_type x3 -> x1, other arithmetic: 6.57 us -> 3.88 us  [per_device(): return result.reshape(4, 2048, LANES).astype(F32)]
  transfers between devices with their start and end apart: 2 -> 0, of which waited for: 2 -> 0; matrix products, arithmetic and copies ran while one was open for 0% -> 0% of each run, Pallas kernels for 0% -> 0%
where the time goes in v1:
time: 113 us
  Pallas kernels  109 us (96%)
  other arithmetic  3.88 us (3%)
    pallas_call x1, Pallas kernels, per_device(): pl.pallas_call(body, out_shape=jax.ShapeDtypeStruct((4, SIDE, SIDE, CORES...  109 us
    convert_element_type x1, other arithmetic, per_device(): return result.reshape(4, 2048, LANES).astype(F32)  3.88 us

profile of v1, /device:TPU:2, one launch (start us, length us, event | category | flops | bytes accessed | tf_op | source)
XLA Modules:
  0.0 112.6 jit_solution(15066062053904137600)
XLA Ops:
  0.0 108.7 %screen_contract.1 = bf16[4,4,4,2,4,16,128]{6,5,4,3,2,1,0:T(8,128)(2,1)} custom-call(f32[128,64,128]{2,1,0:T(8,128)} %x_ref.1, s32[4,16]{1,0:T(4,128)} %bitcast.4, bf16[1024,128]{1,0:T(8,128)(2,1)} %metric_ref.1), custom_call_target="tpu_custom_call" | custom-call | tf_op jit(solution)/shard_map/screen_contract/pallas_call | solution.py:217
  108.7 3.9 %bitcast_convert_fusion = f32[4,2048,128]{2,1,0:T(8,128)} fusion(bf16[4,4,4,2,4,16,128]{6,5,4,3,2,1,0:T(8,128)(2,1)} %screen_contract.1), kind=kLoop, calls=%fused_computation | loop fusion | flops 1048576 | bytes 6291456 | tf_op jit(solution)/shard_map/convert_element_type | solution.py:242

commit v2 on v1

v2 whole, which is shorter than its diff:
```python
import jax
import jax.numpy as jnp
from jax import lax
from jax.experimental import pallas as pl
from jax.experimental.pallas import tpu as pltpu
from jax.sharding import PartitionSpec as P

MESH = pl.DeviceIdType.MESH
BF = jnp.bfloat16
F32 = jnp.float32
SIDE, CORES, DEPTH = 4, 2, 8
WIDE = SIDE * SIDE * CORES
CHIPS = SIDE * SIDE
LANES = 128
PAIR = 2

OFFSETS = (
    (0, 0), (1, 0), (-1, 0), (0, 1), (0, -1), (1, 1), (-1, -1), (-1, 1),
    (1, -1), (2, 0), (0, 2), (2, 1), (1, 2), (2, -1), (-1, 2), (2, 2),
)
Z_ORDER = (4, 3, 5, 2, 6, 1, 7)
METRIC_FROM = 8
NEAR = 4
EARLY = 8
UNITS_FROM = 9


def pick(index, table):
    total = jnp.int32(0)
    for k, value in enumerate(table):
        if value:
            total = total + jnp.where(index == k, jnp.int32(value), jnp.int32(0))
    return total


def body(
    x_ref, mask_ref, metric_ref, out_ref,
    ob, xf, xb, rb, sb, ab, mb, yb,
    load_sem, own_sem, s1_send, s1_recv, a_send, a_recv, b_send, b_recv,
    mz_send, mz_recv, mm_send, mm_recv, mc_send, mc_recv,
):
    w = lax.axis_index("wide")
    z = lax.axis_index("narrow")
    core = lax.rem(w, 2)
    xx = lax.rem(w // 2, SIDE)
    yy = w // (2 * SIDE)
    half, quarter = z // 4, lax.rem(z, 4)

    def chip_at(dx, dy):
        return lax.rem(yy + dy + SIDE, SIDE) * SIDE + lax.rem(xx + dx + SIDE, SIDE)

    def load(g):
        dx, dy = OFFSETS[g]
        rows = pl.ds(chip_at(dx, dy) * 8, 8)
        return pltpu.make_async_copy(x_ref.at[rows], xf.at[rows], load_sem.at[g])

    barrier = pltpu.get_barrier_semaphore()
    for k in Z_ORDER:
        pl.semaphore_signal(
            barrier, inc=1, device_id=(w, lax.rem(z + k, DEPTH)), device_id_type=MESH
        )
    for g in range(CHIPS - 1, -1, -1):
        dx, dy = OFFSETS[g]
        for dc in (0, 1):
            if g == 0 and dc == 0:
                continue
            pl.semaphore_signal(
                barrier, inc=1,
                device_id=(chip_at(dx, dy) * 2 + lax.rem(core + dc, 2), z),
                device_id_type=MESH,
            )

    for g in range(CHIPS):
        load(g).start()

    def convert(g):
        dx, dy = OFFSETS[g]
        first = chip_at(dx, dy) * 8
        load(g).wait()
        xb[pl.ds(first, 8)] = xf[pl.ds(first, 8)].astype(BF)

    def masked(block, weight):
        return (block.astype(F32) * weight).astype(BF).reshape(4, 16, LANES)

    for g in range(EARLY):
        convert(g)
    for m in range(4):
        weight = mask_ref[m, w // 2].astype(F32)
        sb[0, pl.ds((m // 2) * 4, 4), m % 2, core] = masked(xb[w * 4 + m], weight)
    pl.semaphore_wait(barrier, DEPTH - 1 + WIDE - 1)

    my_lanes = pl.ds(pl.multiple_of(z * LANES, LANES), LANES)

    def deep_send(g, cores=slice(None)):
        place = ab.at[g, :, cores, :, my_lanes]
        for k in Z_ORDER:
            there = lax.rem(z + k, DEPTH)
            pltpu.make_async_remote_copy(
                sb.at[g, there, :, cores], place, a_send, a_recv.at[g],
                device_id=(w, there), device_id_type=MESH,
            ).start()
        pltpu.make_async_copy(sb.at[g, z, :, cores], place, a_recv.at[g]).start()

    deep_send(0, pl.ds(core, 1))

    my_rows = pl.ds(pl.multiple_of(w * 32, 32), 32)

    def metric_start():
        pltpu.make_async_copy(metric_ref.at[my_rows], mb.at[w, :, my_lanes], mz_recv).start()
        for k in Z_ORDER:
            pltpu.make_async_remote_copy(
                metric_ref.at[my_rows], mb.at[w, :, my_lanes], mz_send, mz_recv,
                device_id=(w, lax.rem(z + k, DEPTH)), device_id_type=MESH,
            ).start()

    def plane_send(g, dc):
        dx, dy = OFFSETS[g]
        there = chip_at(dx, dy) * 2 + lax.rem(core + dc, 2)
        pltpu.make_async_remote_copy(
            xb.at[pl.ds(there * 4, 4)], rb.at[g, core], s1_send, s1_recv.at[g, core],
            device_id=(there, z), device_id_type=MESH,
        ).start()

    def metric_send(g):
        dx, dy = OFFSETS[g]
        pltpu.make_async_remote_copy(
            mb.at[w], mb.at[w], mm_send, mm_recv.at[g],
            device_id=(chip_at(dx, dy) * 2 + core, z), device_id_type=MESH,
        ).start()

    def metric_across(source):
        pltpu.make_async_remote_copy(
            mb.at[source], mb.at[source], mc_send, mc_recv,
            device_id=(w + 1 - 2 * core, z), device_id_type=MESH,
        ).start()

    def screen(g, dc):
        dx, dy = OFFSETS[g]
        chip = chip_at(-dx, -dy)
        c = lax.rem(core + dc, 2)
        arrived = rb.at[g, c]
        pltpu.make_async_copy(arrived, arrived, s1_recv.at[g, c]).wait()
        for m in range(4):
            weight = mask_ref[m, chip].astype(F32)
            sb[g, pl.ds((m // 2) * 4, 4), m % 2, c] = masked(rb[g, c, m], weight)

    def core_send(g, dc):
        deep_send(g, pl.ds(lax.rem(core + dc, 2), 1))

    def metric_arrived(k):
        dx, dy = OFFSETS[k]
        source = chip_at(-dx, -dy) * 2 + core
        pltpu.make_async_copy(mb.at[source], mb.at[source], mm_recv.at[k]).wait()
        metric_across(source)

    units = [(g, dc) for dc in (0, 1) for g in range(1, NEAR + 1)]
    units_all = list(units)
    pending = []
    plane_send(0, 1)
    for g, dc in units:
        plane_send(g, dc)
    metric_start()
    screen(0, 1)
    for g in range(NEAR + 1, CHIPS):
        if g >= EARLY:
            convert(g)
        plane_send(g, 0)
        plane_send(g, 1)
        if g == NEAR + 1:
            core_send(0, 1)
        if g == METRIC_FROM:
            pltpu.make_async_copy(mb.at[w], mb.at[w], mz_recv).wait()
            metric_across(w)
        if g > METRIC_FROM:
            metric_send(g - METRIC_FROM)
        if g > UNITS_FROM and units:
            screen(*units.pop(0))
            pending.append(units_all.pop(0))
            if len(pending) > 1:
                core_send(*pending.pop(0))
    for g in range(CHIPS - METRIC_FROM, CHIPS):
        metric_send(g)
    for unit in units:
        screen(*unit)
        pending.append(unit)
        core_send(*pending.pop(0))
    for g in range(NEAR + 1, CHIPS):
        screen(g, 0)
        screen(g, 1)
        if g == NEAR + 1:
            core_send(*pending.pop(0))
        else:
            deep_send(g - 1)
        if g > METRIC_FROM:
            metric_arrived(g - METRIC_FROM)
    deep_send(CHIPS - 1)
    for k in range(CHIPS - METRIC_FROM, CHIPS):
        metric_arrived(k)
    pltpu.make_async_copy(mb.at[pl.ds(0, CHIPS)], mb.at[pl.ds(0, CHIPS)], mc_recv).wait()

    dxs = [dx % SIDE for dx, _ in OFFSETS]
    dys = [dy % SIDE for _, dy in OFFSETS]

    def result_send(g):
        xs = lax.rem(xx - pick(g, dxs) + SIDE, SIDE)
        ys = lax.rem(yy - pick(g, dys) + SIDE, SIDE)
        place = ob.at[pl.ds(half * 2, 2), ys, xs, :, quarter]
        pltpu.make_async_copy(yb.at[g, :, :, :, my_lanes], place, b_recv.at[g]).start()
        for k in Z_ORDER:
            there = lax.rem(z + k, DEPTH)
            lanes = pl.ds(pl.multiple_of(there * LANES, LANES), LANES)
            pltpu.make_async_remote_copy(
                yb.at[g, :, :, :, lanes], place, b_send, b_recv.at[g],
                device_id=(w, there), device_id_type=MESH,
            ).start()

    def contract(step):
        for i in range(PAIR):
            g = step * PAIR + i
            pltpu.make_async_copy(ab.at[g], ab.at[g], a_recv.at[g]).wait()
        rows = ab[pl.ds(step * PAIR, PAIR)].reshape(PAIR * 64, 1024)
        product = jnp.dot(rows, mb[...].reshape(1024, 1024), preferred_element_type=F32)
        yb[pl.ds(step * PAIR, PAIR)] = product.astype(BF).reshape(PAIR, 2, 2, 16, 1024)

    contract(0)

    @pl.loop(1, CHIPS // PAIR)
    def _(step):
        contract(step)
        for i in range(PAIR):
            result_send((step - 1) * PAIR + i)

    for i in range(PAIR):
        result_send(CHIPS - PAIR + i)

    def drain(ref, sem):
        pltpu.make_async_copy(ref, ref, sem).wait()

    drain(xb.at[pl.ds(0, 124)], s1_send)
    drain(mb.at[0, :, pl.ds(0, 7 * LANES)], mz_send)
    drain(mb.at[pl.ds(0, 15)], mm_send)
    drain(mb.at[pl.ds(0, 16)], mc_send)
    drain(sb.at[:, pl.ds(0, 7)], a_send)
    drain(yb.at[:, :, :, :, pl.ds(0, 7 * LANES)], b_send)

    @pl.loop(0, CHIPS)
    def _(g):
        xs = lax.rem(xx - pick(g, dxs) + SIDE, SIDE)
        ys = lax.rem(yy - pick(g, dys) + SIDE, SIDE)
        landed = ob.at[:, ys, xs]
        pltpu.make_async_copy(landed, landed, b_recv.at[g]).wait()
        out_ref[:, ys, xs] = landed[...].astype(F32)


def per_device(three_centre, screen_mask, metric):
    dma = pltpu.SemaphoreType.DMA
    result = pl.pallas_call(
        body,
        out_shape=pltpu.VMEM((4, SIDE, SIDE, CORES, 4, 16, LANES), F32),
        in_specs=[
            pl.BlockSpec(memory_space=pl.ANY),
            pl.BlockSpec(memory_space=pltpu.SMEM),
            pl.BlockSpec(memory_space=pl.ANY),
        ],
        out_specs=pl.BlockSpec(memory_space=pltpu.VMEM),
        scratch_shapes=[
            pltpu.VMEM((4, SIDE, SIDE, CORES, 4, 16, LANES), BF),
            pltpu.VMEM((128, 64, LANES), F32),
            pltpu.VMEM((128, 64, LANES), BF),
            pltpu.VMEM((CHIPS, CORES, 4, 64, LANES), BF),
            pltpu.VMEM((CHIPS, DEPTH, 2, 2, 16, LANES), BF),
            pltpu.VMEM((CHIPS, 2, 2, 16, 1024), BF),
            pltpu.VMEM((WIDE, 32, 1024), BF),
            pltpu.VMEM((CHIPS, 2, 2, 16, 1024), BF),
            dma((CHIPS,)), dma, dma, dma((CHIPS, CORES)), dma, dma((CHIPS,)), dma, dma((CHIPS,)),
            dma, dma, dma, dma((CHIPS,)), dma, dma,
        ],
        compiler_params=pltpu.CompilerParams(
            collective_id=0, has_side_effects=True, vmem_limit_bytes=56 * 1024 * 1024
        ),
        name="screen_contract",
    )(three_centre, screen_mask.reshape(4, 16), metric)
    return result.reshape(4, 2048, LANES)


def solution(mesh):
    in_specs = (P(None, "wide", "narrow"), P("wide", None, "narrow"), P(None, "narrow"))
    out_specs = P("wide", None, "narrow")
    return jax.shard_map(
        per_device, mesh=mesh, in_specs=in_specs, out_specs=out_specs, check_vma=False
    )
```

time: 113 us -> 108 us (0.956)
  Pallas kernels: 109 us -> 105 us
  other arithmetic: 3.88 us -> 0 us
  local copies, waits for them, and re-layouts: 0 us -> 2.02 us
    convert_element_type x1 -> x0, other arithmetic: 3.88 us -> none  [per_device(): return result.reshape(4, 2048, LANES).astype(F32)]
    pallas_call x1, Pallas kernels: 109 us -> 105 us  [per_device(): pl.pallas_call(body, out_shape=pltpu.VMEM((4, SIDE, SIDE, CORES, 4, 16, L...]
    unnamed x0 -> x1, local copies, waits for them, and re-layouts: none -> 2.02 us
where the time goes in v2:
time: 108 us; the launch traced here: 107 us
  Pallas kernels  105 us (97%)
  local copies, waits for them, and re-layouts  2.02 us (2%)
    pallas_call x1, Pallas kernels, per_device(): pl.pallas_call(body, out_shape=pltpu.VMEM((4, SIDE, SIDE, CORES, 4, 16, L...  105 us

profile of v2, /device:TPU:2, one launch (start us, length us, event | category | flops | bytes accessed | tf_op | source)
XLA Modules:
  0.0 107.2 jit_solution(8403976389715417642)
XLA Ops:
  0.0 105.2 %screen_contract.1 = f32[4,4,4,2,4,16,128]{6,5,4,3,2,1,0:T(8,128)S(1)} custom-call(f32[128,64,128]{2,1,0:T(8,128)} %x_ref.1, s32[4,16]{1,0:T(4,128)} %bitcast.3, bf16[1024,128]{1,0:T(8,128)(2,1)} %metric_ref.1), custom_call_target="tpu_custom_call" | custom-call | tf_op jit(solution)/shard_map/screen_contract/pallas_call | solution.py:257
  105.2 2.0 %copy.5 = f32[4,2048,128]{2,1,0:T(8,128)} copy(f32[4,2048,128]{2,1,0:T(8,128)S(1)} %bitcast.2) | data formatting | bytes 8388608

commit v3 on v2

--- a/solution.py
+++ b/solution.py
@@ -21,6 +21,7 @@
 Z_ORDER = (4, 3, 5, 2, 6, 1, 7)
 METRIC_FROM = 8
 NEAR = 4
+FURTHER = (5, 11, 15)
 EARLY = 8
 UNITS_FROM = 9
 
@@ -37,7 +38,7 @@
     x_ref, mask_ref, metric_ref, out_ref,
     ob, xf, xb, rb, sb, ab, mb, yb,
     load_sem, own_sem, s1_send, s1_recv, a_send, a_recv, b_send, b_recv,
-    mz_send, mz_recv, mm_send, mm_recv, mc_send, mc_recv,
+    mz_send, mz_recv, mm_send, mm_recv, mc_send, mc_recv, rounds,
 ):
     w = lax.axis_index("wide")
     z = lax.axis_index("narrow")
@@ -59,7 +60,7 @@
         pl.semaphore_signal(
             barrier, inc=1, device_id=(w, lax.rem(z + k, DEPTH)), device_id_type=MESH
         )
-    for g in range(CHIPS - 1, -1, -1):
+    for g in range(NEAR, -1, -1):
         dx, dy = OFFSETS[g]
         for dc in (0, 1):
             if g == 0 and dc == 0:
@@ -70,6 +71,16 @@
                 device_id_type=MESH,
             )
 
+    def tell(r):
+        for g in range(1, NEAR + 1):
+            pl.semaphore_signal(
+                rounds.at[r - 1], inc=1,
+                device_id=(chip_at(*OFFSETS[g]) * 2 + core, z), device_id_type=MESH,
+            )
+
+    def hear(r):
+        pl.semaphore_wait(rounds.at[r - 1], 4)
+
     for g in range(CHIPS):
         load(g).start()
 
@@ -87,7 +98,8 @@
     for m in range(4):
         weight = mask_ref[m, w // 2].astype(F32)
         sb[0, pl.ds((m // 2) * 4, 4), m % 2, core] = masked(xb[w * 4 + m], weight)
-    pl.semaphore_wait(barrier, DEPTH - 1 + WIDE - 1)
+    pl.semaphore_wait(barrier, DEPTH - 1 + 1 + 2 * NEAR)
+    tell(1)
 
     my_lanes = pl.ds(pl.multiple_of(z * LANES, LANES), LANES)
 
@@ -164,6 +176,11 @@
     for g in range(NEAR + 1, CHIPS):
         if g >= EARLY:
             convert(g)
+        if g in FURTHER:
+            r = FURTHER.index(g) + 1
+            hear(r)
+            if r < len(FURTHER):
+                tell(r + 1)
         plane_send(g, 0)
         plane_send(g, 1)
         if g == NEAR + 1:
@@ -274,6 +291,7 @@
             pltpu.VMEM((CHIPS, 2, 2, 16, 1024), BF),
             dma((CHIPS,)), dma, dma, dma((CHIPS, CORES)), dma, dma((CHIPS,)), dma, dma((CHIPS,)),
             dma, dma, dma, dma((CHIPS,)), dma, dma,
+            pltpu.SemaphoreType.REGULAR((3,)),
         ],
         compiler_params=pltpu.CompilerParams(
             collective_id=0, has_side_effects=True, vmem_limit_bytes=56 * 1024 * 1024

time: 108 us -> 105 us (0.972); the launches traced: 107 us -> 105 us
  Pallas kernels: 105 us -> 103 us
    pallas_call x1, Pallas kernels: 105 us -> 103 us  [per_device(): pl.pallas_call(body, out_shape=pltpu.VMEM((4, SIDE, SIDE, CORES, 4, 16, L...]
where the time goes in v3:
time: 105 us
  Pallas kernels  103 us (98%)
  local copies, waits for them, and re-layouts  2.02 us (2%)
    pallas_call x1, Pallas kernels, per_device(): pl.pallas_call(body, out_shape=pltpu.VMEM((4, SIDE, SIDE, CORES, 4, 16, L...  103 us

profile of v3, /device:TPU:2, one launch (start us, length us, event | category | flops | bytes accessed | tf_op | source)
XLA Modules:
  0.0 105.3 jit_solution(12657264492940129980)
XLA Ops:
  0.0 103.3 %screen_contract.1 = f32[4,4,4,2,4,16,128]{6,5,4,3,2,1,0:T(8,128)S(1)} custom-call(f32[128,64,128]{2,1,0:T(8,128)} %x_ref.1, s32[4,16]{1,0:T(4,128)} %bitcast.3, bf16[1024,128]{1,0:T(8,128)(2,1)} %metric_ref.1), custom_call_target="tpu_custom_call" | custom-call | tf_op jit(solution)/shard_map/screen_contract/pallas_call | solution.py:274
  103.3 2.0 %copy.5 = f32[4,2048,128]{2,1,0:T(8,128)} copy(f32[4,2048,128]{2,1,0:T(8,128)S(1)} %bitcast.2) | data formatting | bytes 8388608

commit v4 on v3

--- a/solution.py
+++ b/solution.py
@@ -21,9 +21,9 @@
 Z_ORDER = (4, 3, 5, 2, 6, 1, 7)
 METRIC_FROM = 8
 NEAR = 4
-FURTHER = (5, 11, 15)
+FURTHER = (5, 11)
 EARLY = 8
-UNITS_FROM = 9
+UNITS_FROM = 5
 
 
 def pick(index, table):
@@ -72,7 +72,7 @@
             )
 
     def tell(r):
-        for g in range(1, NEAR + 1):
+        for g in range(1, NEAR + 1) if r == 1 else range(NEAR + 1, 2 * NEAR + 1):
             pl.semaphore_signal(
                 rounds.at[r - 1], inc=1,
                 device_id=(chip_at(*OFFSETS[g]) * 2 + core, z), device_id_type=MESH,
@@ -291,7 +291,7 @@
             pltpu.VMEM((CHIPS, 2, 2, 16, 1024), BF),
             dma((CHIPS,)), dma, dma, dma((CHIPS, CORES)), dma, dma((CHIPS,)), dma, dma((CHIPS,)),
             dma, dma, dma, dma((CHIPS,)), dma, dma,
-            pltpu.SemaphoreType.REGULAR((3,)),
+            pltpu.SemaphoreType.REGULAR((2,)),
         ],
         compiler_params=pltpu.CompilerParams(
             collective_id=0, has_side_effects=True, vmem_limit_bytes=56 * 1024 * 1024

time: 105 us -> 105 us (level)
  no operation moved by 1% of the time
where the time goes in v4:
time: 105 us
  Pallas kernels  103 us (98%)
  local copies, waits for them, and re-layouts  2.02 us (2%)
    pallas_call x1, Pallas kernels, per_device(): pl.pallas_call(body, out_shape=pltpu.VMEM((4, SIDE, SIDE, CORES, 4, 16, L...  103 us

profile of v4, /device:TPU:2, one launch (start us, length us, event | category | flops | bytes accessed | tf_op | source)
XLA Modules:
  0.0 105.1 jit_solution(11310881272559248369)
XLA Ops:
  0.0 103.1 %screen_contract.1 = f32[4,4,4,2,4,16,128]{6,5,4,3,2,1,0:T(8,128)S(1)} custom-call(f32[128,64,128]{2,1,0:T(8,128)} %x_ref.1, s32[4,16]{1,0:T(4,128)} %bitcast.3, bf16[1024,128]{1,0:T(8,128)(2,1)} %metric_ref.1), custom_call_target="tpu_custom_call" | custom-call | tf_op jit(solution)/shard_map/screen_contract/pallas_call | solution.py:274
  103.1 2.0 %copy.5 = f32[4,2048,128]{2,1,0:T(8,128)} copy(f32[4,2048,128]{2,1,0:T(8,128)S(1)} %bitcast.2) | data formatting | bytes 8388608
